TPU v7x, 32 devices: a whole 2x2x4 slice. The times are simulated.
32 devices in a mesh: frames: 8 (over z, core), heads: 4 (over y, x).
Axes of the slice: x: 2, y: 2, z: 4, core: 2. Of those that a mesh axis runs over, the one named last changes fastest.
Arguments:
- clip: bfloat16 [16, 8, 128, 320], P('frames', 'heads'), may hold values from -6 to 6
- w_time: bfloat16 [3, 320, 320], replicated, may hold values from -0.1875 to 0.1875
- w_down: bfloat16 [320, 1280], replicated, may hold values from -0.3125 to 0.3125
- w_embed: bfloat16 [320, 1280], replicated, may hold values from -0.3125 to 0.3125
- w_qkv: bfloat16 [1280, 3840], P(None, 'heads'), may hold values from -0.15625 to 0.15625
- w_out: bfloat16 [1280, 1280], P('heads'), may hold values from -0.15625 to 0.15625
- w_up: bfloat16 [1280, 320], replicated, may hold values from -0.15625 to 0.15625
- timestep: int32 [1], replicated, may hold values from 0 to 999
- cotangent: bfloat16 [16, 8, 128, 320], P('frames', 'heads'), may hold values from -6 to 6
Outputs:
- output: bfloat16 [16, 8, 128, 320], P('frames', 'heads')
- grad_clip: float32 [16, 8, 128, 320], P('frames', 'heads')
- grad_time: float32 [3, 320, 320], replicated
- grad_down: float32 [320, 1280], replicated
- grad_embed: float32 [320, 1280], replicated
- grad_qkv: float32 [1280, 3840], P(None, 'heads')
- grad_out: float32 [1280, 1280], P('heads')
- grad_up: float32 [1280, 320], replicated
All inputs are finite; a program needn't handle non-finite values.
Results may differ from a plain program's by a relative error of at most 0.024.
Values may be sent and summed in bfloat16 or wider, within the bound.
No kernel may reach another device: no remote copies, remote signals or barrier semaphores. Data moves between devices by JAX's collectives and lax.ppermute only.
A program may use at most 128 MiB of HBM per device.

v0:
```python
import math
import jax
import jax.numpy as jnp
from jax import lax
from jax.sharding import PartitionSpec as P

HD = 80


def extended(cells, sides, width):
    for axis, dim in sides:
        count = lax.axis_size(axis)
        ends = count - 1
        head = lax.slice_in_dim(cells, 0, width, axis=dim)
        tail = lax.slice_in_dim(cells, cells.shape[dim] - width, cells.shape[dim], axis=dim)
        cells = jnp.concatenate(
            [
                lax.ppermute(tail, axis, [(i, (i + 1) % count) for i in range(ends)]),
                cells,
                lax.ppermute(head, axis, [((i + 1) % count, i) for i in range(ends)]),
            ],
            axis=dim,
        )
    return cells


def matmul(left, right):
    return jnp.dot(left, right, preferred_element_type=jnp.float32)


def inner_rows(left, right):
    return lax.dot_general(
        left, right, (((0,), (0,)), ((), ())), preferred_element_type=jnp.float32
    )


def inner_cols(left, right):
    return lax.dot_general(
        left, right, (((1,), (1,)), ((), ())), preferred_element_type=jnp.float32
    )


def upsample(field):
    return jnp.repeat(jnp.repeat(jnp.repeat(field, 2, 0), 2, 1), 2, 2)


def time_embed(timestep, width):
    half = width // 2
    freqs = jnp.exp(-math.log(10000.0) * jnp.arange(half, dtype=jnp.float32) / half)
    angle = timestep.astype(jnp.float32)[0] * freqs
    return jax.nn.silu(jnp.concatenate([jnp.cos(angle), jnp.sin(angle)])).astype(jnp.bfloat16)


def to_coarse(field):
    local = lax.all_to_all(field, "frames", split_axis=2, concat_axis=0, tiled=True)
    whole = lax.all_gather(local, "heads", axis=1, tiled=True)
    return (local, whole)


def coarse_sum(partial_value):
    return lax.psum_scatter(
        partial_value.astype(jnp.bfloat16), "heads", scatter_dimension=1, tiled=True
    ).astype(jnp.float32)


def to_fine(field):
    return lax.all_to_all(field, "frames", split_axis=0, concat_axis=2, tiled=True)


def shards(clip, w_time, w_down, w_embed, w_qkv, w_out, w_up, timestep, cotangent):
    frames, rows, columns, chans = clip.shape
    width = w_down.shape[1]
    half_f, half_r, half_c = (frames // 2, rows // 2, columns // 2)
    scale = 1.0 / math.sqrt(HD)
    padded = extended(clip, (("frames", 0),), 1)
    branch = jnp.zeros((frames * rows * columns, chans), jnp.float32)
    for tap in range(3):
        branch = branch + matmul(padded[tap : tap + frames].reshape(-1, chans), w_time[tap])
    hidden = (clip.astype(jnp.float32).reshape(-1, chans) + branch).astype(jnp.bfloat16)
    hidden_f = hidden.astype(jnp.float32).reshape(frames, rows, columns, chans)
    pooled = hidden_f.reshape(half_f, 2, half_r, 2, half_c, 2, chans).mean(axis=(1, 3, 5))
    pooled = pooled.astype(jnp.bfloat16).reshape(-1, chans)
    embed = time_embed(timestep, w_embed.shape[0])
    shift = matmul(embed[None, :], w_embed)
    coarse_in = (matmul(pooled, w_down) + shift).astype(jnp.bfloat16)
    coarse_in = coarse_in.reshape(half_f, 1, half_r * half_c, width)
    local_in, full_in = to_coarse(coarse_in)
    coarse_frames, groups, per_group = (full_in.shape[0], full_in.shape[1], full_in.shape[2])
    places = groups * per_group
    token_mat = full_in.reshape(-1, width)
    heads_here = w_qkv.shape[1] // (3 * HD)
    qkv = (
        matmul(token_mat, w_qkv)
        .astype(jnp.bfloat16)
        .reshape(coarse_frames, places, heads_here, 3, HD)
    )
    query = qkv[:, :, :, 0]
    keys = qkv[:, :, :, 1]
    values = qkv[:, :, :, 2]
    scores = jnp.einsum("tpnd,spnd->ntsp", query, keys, preferred_element_type=jnp.float32) * scale
    probs = jax.nn.softmax(scores, axis=2)
    weights = probs.astype(jnp.bfloat16)
    attended = jnp.einsum("ntsp,spnd->tpnd", weights, values, preferred_element_type=jnp.float32)
    attended = attended.astype(jnp.bfloat16).reshape(-1, heads_here * HD)
    mixed = coarse_sum(matmul(attended, w_out).reshape(coarse_frames, groups, per_group, width))
    coarse_out = (local_in.astype(jnp.float32) + mixed).astype(jnp.bfloat16)
    fine_back = to_fine(coarse_out).reshape(-1, width)
    lifted = matmul(fine_back, w_up).reshape(half_f, half_r, half_c, chans)
    output = (hidden_f + upsample(lifted)).astype(jnp.bfloat16)
    upstream = cotangent.astype(jnp.float32)
    pooled_grad = upstream.reshape(half_f, 2, half_r, 2, half_c, 2, chans).sum(axis=(1, 3, 5))
    pooled_grad = pooled_grad.astype(jnp.bfloat16).reshape(-1, chans)
    grad_up_part = inner_rows(fine_back, pooled_grad)
    back_in = (
        inner_cols(pooled_grad, w_up)
        .astype(jnp.bfloat16)
        .reshape(half_f, 1, half_r * half_c, width)
    )
    local_grad, full_grad = to_coarse(back_in)
    grad_mat = full_grad.reshape(-1, width)
    grad_out_part = inner_rows(attended, grad_mat)
    attend_grad = inner_cols(grad_mat, w_out).astype(jnp.bfloat16)
    attend_grad = attend_grad.reshape(coarse_frames, places, heads_here, HD)
    weight_grad = jnp.einsum(
        "tpnd,spnd->ntsp", attend_grad, values, preferred_element_type=jnp.float32
    )
    score_grad = probs * (weight_grad - jnp.sum(probs * weight_grad, axis=2, keepdims=True)) * scale
    score_grad = score_grad.astype(jnp.bfloat16)
    query_grad = jnp.einsum("ntsp,spnd->tpnd", score_grad, keys, preferred_element_type=jnp.float32)
    keys_grad = jnp.einsum("ntsp,tpnd->spnd", score_grad, query, preferred_element_type=jnp.float32)
    values_grad = jnp.einsum(
        "ntsp,tpnd->spnd", weights, attend_grad, preferred_element_type=jnp.float32
    )
    qkv_grad = jnp.stack([query_grad, keys_grad, values_grad], axis=3).astype(jnp.bfloat16)
    qkv_grad = qkv_grad.reshape(-1, heads_here * 3 * HD)
    grad_qkv_part = inner_rows(token_mat, qkv_grad)
    input_grad = coarse_sum(
        inner_cols(qkv_grad, w_qkv).reshape(coarse_frames, groups, per_group, width)
    )
    coarse_grad = (input_grad + local_grad.astype(jnp.float32)).astype(jnp.bfloat16)
    fine_grad = to_fine(coarse_grad).reshape(-1, width)
    column_sum = jnp.sum(fine_grad.astype(jnp.float32), axis=0)
    grad_down_part = inner_rows(pooled, fine_grad)
    spread = inner_cols(fine_grad, w_down).reshape(half_f, half_r, half_c, chans)
    hidden_grad = (upstream + upsample(spread) * 0.125).astype(jnp.bfloat16)
    grad_padded = extended(hidden_grad, (("frames", 0),), 1)
    flat_grad = hidden_grad.reshape(-1, chans)
    grad_clip = flat_grad.astype(jnp.float32)
    taps = []
    for tap in range(3):
        grad_clip = grad_clip + inner_cols(
            grad_padded[2 - tap : 2 - tap + frames].reshape(-1, chans), w_time[tap]
        )
        taps.append(inner_rows(padded[tap : tap + frames].reshape(-1, chans), flat_grad))
    grad_clip = grad_clip.reshape(frames, rows, columns, chans)
    coarse_sums = (
        lax.psum(grad_qkv_part.astype(jnp.bfloat16), "frames").astype(jnp.float32),
        lax.psum(grad_out_part.astype(jnp.bfloat16), "frames").astype(jnp.float32),
    )
    fine_sums = lax.psum(
        (jnp.stack(taps), grad_down_part, grad_up_part, column_sum), ("frames", "heads")
    )
    grad_embed = embed.astype(jnp.float32)[:, None] * fine_sums[3][None, :]
    return (
        output,
        grad_clip,
        fine_sums[0],
        fine_sums[1],
        grad_embed,
        coarse_sums[0],
        coarse_sums[1],
        fine_sums[2],
    )


def solution(mesh):
    return jax.shard_map(
        shards,
        mesh=mesh,
        in_specs=(
            P("frames", "heads", None, None),
            P(),
            P(),
            P(),
            P(None, "heads"),
            P("heads", None),
            P(),
            P(),
            P("frames", "heads", None, None),
        ),
        out_specs=(
            P("frames", "heads", None, None),
            P("frames", "heads", None, None),
            P(),
            P(),
            P(),
            P(None, "heads"),
            P("heads", None),
            P(),
        ),
        check_vma=False,
    )
```

profile of v0, /device:TPU:0, one launch (start us, length us, event | category | flops | bytes accessed | tf_op | source)
XLA Modules:
  0.0 432.7 jit_solution(15819610578393598799)
XLA Ops:
  7.2 1.9 fusion.68
  9.1 3.1 collective-permute-start
  20.1 7.6 %all-to-all-start.2 = ((bf16[8,2,5120]{2,1,0:T(2,128)(2,1)}), bf16[8,2,5120]{2,1,0:T(2,128)(2,1)}, u32[]{:S(2)}, u32[]{:S(2)}) async-start(bf16[8,2,5120]{2,1,0:T(2,128)(2,1)} %reshape.238), calls=%async_computation.2 | async-start | bytes 327680 | tf_op jit(solution)/shard_map/all_to_all | solution.py:55
  34.0 1.9 reshape.205
  35.9 1.6 constant_dynamic-update-slice_fusion.2
  39.6 1.8 reshape.206
  45.7 2.5 reshape_reshape.3
  53.8 5.1 %all-to-all-start = ((bf16[8,2,5120]{2,1,0:T(2,128)(2,1)}), bf16[8,2,5120]{2,1,0:T(2,128)(2,1)}, u32[]{:S(2)}, u32[]{:S(2)}) async-start(bf16[8,2,5120]{2,1,0:T(2,128)(2,1)} %reshape.236), calls=%async_computation | async-start | bytes 327680 | tf_op jit(solution)/shard_map/all_to_all | solution.py:55
  58.9 2.2 reshape.239
  62.1 11.6 %all_gather.7 = bf16[8,4,8,1280]{3,2,0,1:T(8,128)(2,1)S(1)} all-gather(bf16[8,1,8,1280]{3,2,0,1:T(8,128)(2,1)S(1)} %bitcast.199), channel_id=1, replica_groups=mesh['frames'=8,'heads'=4] {'heads'}, dimensions={1}, use_global_device_ids=true | all-gather | bytes 819200 | tf_op jit(solution)/shard_map/all_gather | solution.py:56
  77.6 11.5 %all_gather.6 = bf16[8,4,8,1280]{3,2,0,1:T(8,128)(2,1)S(1)} all-gather(bf16[8,1,8,1280]{3,2,0,1:T(8,128)(2,1)S(1)} %bitcast.200), channel_id=1, replica_groups=mesh['frames'=8,'heads'=4] {'heads'}, dimensions={1}, use_global_device_ids=true | all-gather | bytes 819200 | tf_op jit(solution)/shard_map/all_gather | solution.py:56
  91.8 3.3 reshape.210
  95.2 2.0 fusion.66
  101.2 2.2 fusion.9
  105.3 1.7 fusion.15
  108.4 2.2 convolution_bitcast_fusion.1
  110.6 2.2 convolution_bitcast_fusion.2
  113.8 2.3 convolution_convert_fusion.3
  118.6 2.7 convolution_convert_fusion.2
  126.0 2.3 convolution_convert_fusion
  128.3 49.5 %all-reduce.13.cloned.1.call-done = (bf16[8,4,8,1280]{3,2,1,0:T(8,128)(2,1)}, bf16[8,4,8,1280]{3,2,1,0:T(8,128)(2,1)}) async-done(((bf16[8,4,8,1280]{3,2,1,0:T(8,128)(2,1)}, bf16[8,4,8,1280]{3,2,1,0:T(8,128)(2,1)}), (bf16[8,4,8,1280]{3,2,1,0:T(8,128)(2,1)}, bf16[8,4,8,1280]{3,2,1,0:T(8,128)(2,1)})) %all-reduce.13.cloned.1.call-update) | async-done | bytes 1310736
  177.8 2.3 fusion.43
  180.1 4.6 %all-to-all-start.3 = ((bf16[8,1,8,1280]{3,2,1,0:T(8,128)(2,1)}), bf16[8,1,8,1280]{3,2,1,0:T(8,128)(2,1)S(1)}, u32[]{:S(2)}, u32[]{:S(2)}) async-start(bf16[8,1,8,1280]{3,2,1,0:T(8,128)(2,1)} %fusion.43), calls=%async_computation.3 | async-start | bytes 327680 | tf_op jit(solution)/shard_map/all_to_all | solution.py:67
  184.7 2.4 fusion.42
  187.1 6.5 %all-to-all-done.3 = bf16[8,1,8,1280]{3,2,1,0:T(8,128)(2,1)S(1)} async-done(((bf16[8,1,8,1280]{3,2,1,0:T(8,128)(2,1)}), bf16[8,1,8,1280]{3,2,1,0:T(8,128)(2,1)S(1)}, u32[]{:S(2)}, u32[]{:S(2)}) %all-to-all-start.3) | async-done | bytes 163872 | tf_op jit(solution)/shard_map/all_to_all | solution.py:67
  193.5 3.4 all-to-all-start.1
  200.6 5.6 %all-to-all-done.1 = bf16[8,1,8,1280]{3,2,1,0:T(8,128)(2,1)S(1)} async-done(((bf16[8,1,8,1280]{3,2,1,0:T(8,128)(2,1)}), bf16[8,1,8,1280]{3,2,1,0:T(8,128)(2,1)S(1)}, u32[]{:S(2)}, u32[]{:S(2)}) %all-to-all-start.1) | async-done | bytes 163872 | tf_op jit(solution)/shard_map/all_to_all | solution.py:67
  214.0 43.6 %psum.44 = f32[1280]{0:T(1024)S(1)} all-reduce(f32[1280]{0:T(1024)S(1)} %convert_reduce_fusion.1), channel_id=1, replica_groups=mesh['frames'=8,'heads'=4] {'frames','heads'}, use_global_device_ids=true, to_apply=%region_11.12 | all-reduce | flops 1280 | bytes 10240 | tf_op jit(solution)/shard_map/psum | solution.py:160
  259.8 7.7 %all-reduce.11.cloned.1.call-done = (bf16[1280,960]{0,1:T(8,128)(2,1)}, bf16[320,1280]{1,0:T(8,128)(2,1)}) async-done(((bf16[1280,960]{0,1:T(8,128)(2,1)}, bf16[320,1280]{1,0:T(8,128)(2,1)}), (bf16[1280,960]{0,1:T(8,128)(2,1)}, bf16[320,1280]{1,0:T(8,128)(2,1)})) %all-reduce.11.cloned.1.call-update) | async-done | bytes 3276816 | tf_op jit(solution)/shard_map/psum | solution.py:157
  267.4 4.4 %convert_element_type.187 = f32[1280,960]{0,1:T(8,128)} convert(bf16[1280,960]{0,1:T(8,128)(2,1)} %get-tuple-element.59) | non-fusion elementwise | flops 1228800 | bytes 7372800 | tf_op jit(solution)/shard_map/convert_element_type | solution.py:157
  276.5 143.7 %all-reduce.9.cloned.1.call-done = (f32[3,320,320]{2,1,0:T(8,128)}, f32[320,1280]{1,0:T(8,128)}, f32[1280,320]{0,1:T(8,128)}) async-done(((f32[3,320,320]{2,1,0:T(8,128)}, f32[320,1280]{1,0:T(8,128)}, f32[1280,320]{0,1:T(8,128)}), (f32[3,320,320]{2,1,0:T(8,128)}, f32[320,1280]{1,0:T(8,128)}, f32[1280,320]{0,1:T(8,128)})) %all-reduce.9.cloned.1.call-update) | async-done | bytes 4505616 | tf_op jit(solution)/shard_map/psum | solution.py:160
  420.3 2.7 copy.287
  (196 shorter events, 69.6 us)
Async XLA Ops:
  7.2 82.8 %copy-start = (bf16[1280,960]{0,1:T(8,128)(2,1)S(1)}, bf16[1280,960]{0,1:T(8,128)(2,1)}, u32[]{:S(2)}) copy-start(bf16[1280,960]{0,1:T(8,128)(2,1)} %param.13) | copy-start | bytes 7372804
  9.1 21.3 %collective-permute-start = (bf16[1,2,128,320]{2,3,1,0:T(8,128)(2,1)}, bf16[1,2,128,320]{2,3,1,0:T(8,128)(2,1)}, u32[]{:S(2)}, u32[]{:S(2)}) collective-permute-start(bf16[1,2,128,320]{2,3,1,0:T(8,128)(2,1)} %get-tuple-element.73), channel_id=1, source_target_pairs={{0,4},{4,8},{8,12},{12,16},{16,20},{20,24},{24,28},{1,5},{5,9},{9,... | collective-permute-start | bytes 491528 | tf_op jit(solution)/shard_map/ppermute | solution.py:18
  12.1 23.8 %collective-permute-start.1 = (bf16[1,2,128,320]{2,3,1,0:T(8,128)(2,1)}, bf16[1,2,128,320]{2,3,1,0:T(8,128)(2,1)}, u32[]{:S(2)}, u32[]{:S(2)}) collective-permute-start(bf16[1,2,128,320]{2,3,1,0:T(8,128)(2,1)} %get-tuple-element.72), channel_id=1, source_target_pairs={{4,0},{8,4},{12,8},{16,12},{20,16},{24,20},{28,24},{5,1},{9,5},{13... | collective-permute-start | bytes 491528 | tf_op jit(solution)/shard_map/ppermute | solution.py:20
  14.6 13.9 %copy-start.6 = (bf16[2,2,128,320]{2,3,1,0:T(8,128)(2,1)S(1)}, bf16[2,2,128,320]{2,3,1,0:T(8,128)(2,1)}, u32[]{:S(2)}) copy-start(bf16[2,2,128,320]{2,3,1,0:T(8,128)(2,1)} %param.9) | copy-start | bytes 983044
  20.1 33.7 %all-to-all-start.2 = ((bf16[8,2,5120]{2,1,0:T(2,128)(2,1)}), bf16[8,2,5120]{2,1,0:T(2,128)(2,1)}, u32[]{:S(2)}, u32[]{:S(2)}) async-start(bf16[8,2,5120]{2,1,0:T(2,128)(2,1)} %reshape.238), calls=%async_computation.2 | async-start | bytes 327680 | tf_op jit(solution)/shard_map/all_to_all | solution.py:55
  34.0 7.4 %copy-start.12 = (bf16[3,320,320]{2,1,0:T(8,128)(2,1)S(1)}, bf16[3,320,320]{2,1,0:T(8,128)(2,1)}, u32[]{:S(2)}) copy-start(bf16[3,320,320]{2,1,0:T(8,128)(2,1)} %param.10) | copy-start | bytes 1843204
  44.5 5.2 %copy-start.4 = (f32[512,320]{0,1:T(8,128)}, f32[512,320]{0,1:T(8,128)S(1)}, u32[]{:S(2)}) copy-start(f32[512,320]{0,1:T(8,128)S(1)} %fusion.8) | copy-start | bytes 1966084
  49.7 4.1 copy-start.37
  53.8 22.3 %all-to-all-start = ((bf16[8,2,5120]{2,1,0:T(2,128)(2,1)}), bf16[8,2,5120]{2,1,0:T(2,128)(2,1)}, u32[]{:S(2)}, u32[]{:S(2)}) async-start(bf16[8,2,5120]{2,1,0:T(2,128)(2,1)} %reshape.236), calls=%async_computation | async-start | bytes 327680 | tf_op jit(solution)/shard_map/all_to_all | solution.py:55
  58.9 15.7 %copy-start.8 = (bf16[320,1280]{1,0:T(8,128)(2,1)S(1)}, bf16[320,1280]{1,0:T(8,128)(2,1)}, u32[]{:S(2)}) copy-start(bf16[320,1280]{1,0:T(8,128)(2,1)} %param.14) | copy-start | bytes 2457604
  58.9 118.9 %all-reduce.13.cloned.1.call-start = ((), (), s32[]{:S(2)}) async-start(), calls=%async_computation.6 | async-start | bytes 2621440
  77.5 13.3 %copy-start.15 = (bf16[64,1,1,1280]{3,2,1,0:T(2,128)(2,1)}, bf16[64,1,1,1280]{3,2,1,0:T(2,128)(2,1)S(1)}, u32[]{:S(2)}) copy-start(bf16[64,1,1,1280]{3,2,1,0:T(2,128)(2,1)S(1)} %reshape.237) | copy-start | bytes 491524
  98.1 5.3 %copy-start.22 = (bf16[8,32,4,80]{3,2,1,0:T(4,128)(2,1)S(1)}, bf16[8,32,4,80]{3,2,1,0:T(4,128)(2,1)}, u32[]{:S(2)}) copy-start(bf16[8,32,4,80]{3,2,1,0:T(4,128)(2,1)} %reshape.214) | copy-start | bytes 491524
  101.2 3.3 copy-start.26
  107.0 6.8 %copy-start.9 = (bf16[320,1280]{1,0:T(8,128)(2,1)S(1)}, bf16[320,1280]{1,0:T(8,128)(2,1)}, u32[]{:S(2)}) copy-start(bf16[320,1280]{1,0:T(8,128)(2,1)} %param.14) | copy-start | bytes 2457604
  108.4 4.4 %copy-start.33 = (bf16[8,32,4,80]{3,0,2,1:T(8,128)(2,1)S(1)}, bf16[8,32,4,80]{3,0,2,1:T(8,128)(2,1)}, u32[]{:S(2)}) copy-start(bf16[8,32,4,80]{3,0,2,1:T(8,128)(2,1)} %fusion.9) | copy-start | bytes 491524
  112.9 3.2 copy-start.20
  121.4 146.0 %all-reduce.11.cloned.1.call-start = ((), (), s32[]{:S(2)}) async-start(), calls=%async_computation.5 | async-start | bytes 6553600 | tf_op jit(solution)/shard_map/psum | solution.py:157
  122.9 3.1 copy-start.19
  128.3 49.5 %copy-start.14 = (bf16[64,1,1,1280]{3,2,1,0:T(2,128)(2,1)S(1)}, bf16[64,1,1,1280]{3,2,1,0:T(2,128)(2,1)}, u32[]{:S(2)}) copy-start(bf16[64,1,1,1280]{3,2,1,0:T(2,128)(2,1)} %reshape.239) | copy-start | bytes 491524
  128.3 56.4 %copy-start.16 = (bf16[64,1,1,1280]{3,2,1,0:T(2,128)(2,1)S(1)}, bf16[64,1,1,1280]{3,2,1,0:T(2,128)(2,1)}, u32[]{:S(2)}) copy-start(bf16[64,1,1,1280]{3,2,1,0:T(2,128)(2,1)} %copy-done.15) | copy-start | bytes 491524
  128.3 68.7 %copy-start.10 = (bf16[320,1280]{1,0:T(8,128)(2,1)S(1)}, bf16[320,1280]{1,0:T(8,128)(2,1)}, u32[]{:S(2)}) copy-start(bf16[320,1280]{1,0:T(8,128)(2,1)} %param.11) | copy-start | bytes 2457604
  180.1 13.5 %all-to-all-start.3 = ((bf16[8,1,8,1280]{3,2,1,0:T(8,128)(2,1)}), bf16[8,1,8,1280]{3,2,1,0:T(8,128)(2,1)S(1)}, u32[]{:S(2)}, u32[]{:S(2)}) async-start(bf16[8,1,8,1280]{3,2,1,0:T(8,128)(2,1)} %fusion.43), calls=%async_computation.3 | async-start | bytes 327680 | tf_op jit(solution)/shard_map/all_to_all | solution.py:67
  184.7 13.0 %copy-start.31 = (bf16[2,2,128,320]{2,3,1,0:T(8,128)(2,1)S(1)}, bf16[2,2,128,320]{2,3,1,0:T(8,128)(2,1)}, u32[]{:S(2)}) copy-start(bf16[2,2,128,320]{2,3,1,0:T(8,128)(2,1)} %param.17) | copy-start | bytes 983044
  193.5 12.7 %all-to-all-start.1 = ((bf16[8,1,8,1280]{3,2,1,0:T(8,128)(2,1)}), bf16[8,1,8,1280]{3,2,1,0:T(8,128)(2,1)S(1)}, u32[]{:S(2)}, u32[]{:S(2)}) async-start(bf16[8,1,8,1280]{3,2,1,0:T(8,128)(2,1)} %fusion.42), calls=%async_computation.1 | async-start | bytes 327680 | tf_op jit(solution)/shard_map/all_to_all | solution.py:67
  196.9 223.4 %all-reduce.9.cloned.1.call-start = ((), (), s32[]{:S(2)}) async-start(), calls=%async_computation.4 | async-start | bytes 9502720 | tf_op jit(solution)/shard_map/psum | solution.py:160
  199.4 6.9 %copy-start.41 = (bf16[64,320]{1,0:T(8,128)(2,1)S(1)}, bf16[64,320]{1,0:T(8,128)(2,1)}, u32[]{:S(2)}) copy-start(bf16[64,320]{1,0:T(8,128)(2,1)} %copy-done.40) | copy-start | bytes 122884
  200.6 7.2 %copy-start.38 = (f32[64,320]{1,0:T(8,128)S(1)}, f32[64,320]{1,0:T(8,128)}, u32[]{:S(2)}) copy-start(f32[64,320]{1,0:T(8,128)} %copy-done.37) | copy-start | bytes 245764
  211.3 61.8 %collective-permute-start.3 = (bf16[1,2,128,320]{2,3,1,0:T(8,128)(2,1)S(1)}, bf16[1,2,128,320]{2,3,1,0:T(8,128)(2,1)S(1)}, u32[]{:S(2)}, u32[]{:S(2)}) collective-permute-start(bf16[1,2,128,320]{2,3,1,0:T(8,128)(2,1)S(1)} %get-tuple-element.70), channel_id=1, source_target_pairs={{0,4},{4,8},{8,12},{12,16},{16,20},{20,24},{24,28},{1,5},{5,9},{9,... | collective-permute-start | bytes 491528 | tf_op jit(solution)/shard_map/ppermute | solution.py:18
  212.6 60.5 %collective-permute-start.2 = (bf16[1,2,128,320]{2,3,1,0:T(8,128)(2,1)S(1)}, bf16[1,2,128,320]{2,3,1,0:T(8,128)(2,1)S(1)}, u32[]{:S(2)}, u32[]{:S(2)}) collective-permute-start(bf16[1,2,128,320]{2,3,1,0:T(8,128)(2,1)S(1)} %get-tuple-element.71), channel_id=1, source_target_pairs={{4,0},{8,4},{12,8},{16,12},{20,16},{24,20},{28,24},{5,1},{9,5},{13... | collective-permute-start | bytes 491528 | tf_op jit(solution)/shard_map/ppermute | solution.py:20
  267.4 4.4 %copy-start.39 = (bf16[320,1280]{1,0:T(8,128)(2,1)S(1)}, bf16[320,1280]{1,0:T(8,128)(2,1)}, u32[]{:S(2)}) copy-start(bf16[320,1280]{1,0:T(8,128)(2,1)} %get-tuple-element.60) | copy-start | bytes 2457604
  423.0 3.2 copy-start.1
  (23 other events, 35.8 us)
Sparse Core Ops, SparseCore 0:
  121.5 56.2 all-reduce.12
  180.8 86.5 all-reduce.10
  274.1 146.1 all-reduce.8
where the time goes:
time: 434 us; the launch traced here: 433 us
  waiting for transfers between devices  213 us (49%)
  blocking collectives  66.7 us (15%)
  local copies, waits for them, and re-layouts  55 us (13%)
  matrix products  32.1 us (7%)
  starting transfers between devices  27.9 us (6%)
  other arithmetic  22.9 us (5%)
  between operations  15.2 us (4%)
    psum x1, waiting for transfers between devices, shards(): lax.psum((jnp.stack(taps), grad_down_part, grad_up_part, column_sum), ('f...  144 us
    unnamed x4, waiting for transfers between devices  49.5 us
    psum x1, blocking collectives, shards(): lax.psum((jnp.stack(taps), grad_down_part, grad_up_part, column_sum), ('f...  43.6 us
    all_gather x2, blocking collectives, to_coarse(): whole = lax.all_gather(local, 'heads', axis=1, tiled=True)  23.1 us
    unnamed x103, local copies, waits for them, and re-layouts  22.5 us
    all_to_all x2, starting transfers between devices, to_coarse(): lax.all_to_all(field, 'frames', split_axis=2, concat_axis=0, tiled=True)  12.7 us
    all_to_all x2, waiting for transfers between devices, to_fine(): lax.all_to_all(field, 'frames', split_axis=0, concat_axis=2, tiled=True)  12.1 us
    dot_general x8, matrix products, matmul(): return jnp.dot(left, right, preferred_element_type=jnp.float32)  9.45 us
  transfers between devices with their start and end apart: 11, of which 5 were waited for; matrix products, arithmetic and copies ran while one was open for 15% of the time, Pallas kernels for 0%

commit v1 on v0

--- a/solution.py
+++ b/solution.py
@@ -158,7 +158,7 @@
         lax.psum(grad_out_part.astype(jnp.bfloat16), "frames").astype(jnp.float32),
     )
     fine_sums = lax.psum(
-        (jnp.stack(taps), grad_down_part, grad_up_part, column_sum), ("frames", "heads")
+        lax.psum((jnp.stack(taps), grad_down_part, grad_up_part, column_sum), "heads"), "frames"
     )
     grad_embed = embed.astype(jnp.float32)[:, None] * fine_sums[3][None, :]
     return (

time: 434 us -> 526 us (1.21)
  waiting for transfers between devices: 213 us -> 318 us
  blocking collectives: 66.7 us -> 49.8 us
    psum x1 -> x2, waiting for transfers between devices: 144 us -> 205 us  [the longest x1 104 us: shards(): lax.psum((jnp.stack(taps), grad_down_part, grad_up_part, column_sum), 'he...]
    psum x1, waiting for transfers between devices: 7.65 us -> 50.2 us  [shards(): lax.psum(grad_qkv_part.astype(jnp.bfloat16), 'frames').astype(jnp.float32)]
    psum x1 -> x2, blocking collectives: 43.6 us -> 26.8 us  [the longest x1 17.3 us: shards(): lax.psum(lax.psum((jnp.stack(taps), grad_down_part, grad_up_part, column_...]
    unnamed x4 -> x5, waiting for transfers between devices: 49.5 us -> 55.9 us
    unnamed x103 -> x101, local copies, waits for them, and re-layouts: 22.5 us -> 23.4 us
  transfers between devices with their start and end apart: 11 -> 12, of which waited for: 5 -> 6; matrix products, arithmetic and copies ran while one was open for 15% -> 12% of each run, Pallas kernels for 0% -> 0%
where the time goes in v1:
time: 526 us; the launch traced here: 525 us
  waiting for transfers between devices  318 us (60%)
  local copies, waits for them, and re-layouts  55.9 us (11%)
  blocking collectives  49.8 us (9%)
  matrix products  33.9 us (6%)
  starting transfers between devices  28.9 us (5%)
  other arithmetic  22.9 us (4%)
  between operations  15.2 us (3%)
    psum x1, waiting for transfers between devices, shards(): lax.psum((jnp.stack(taps), grad_down_part, grad_up_part, column_sum), 'he...  104 us
    psum x1, waiting for transfers between devices, shards(): lax.psum(lax.psum((jnp.stack(taps), grad_down_part, grad_up_part, column_...  101 us
    unnamed x5, waiting for transfers between devices  55.9 us
    psum x1, waiting for transfers between devices, shards(): lax.psum(grad_qkv_part.astype(jnp.bfloat16), 'frames').astype(jnp.float32)  50.2 us
    unnamed x101, local copies, waits for them, and re-layouts  23.4 us
    all_gather x2, blocking collectives, to_coarse(): whole = lax.all_gather(local, 'heads', axis=1, tiled=True)  23.1 us
    psum x1, blocking collectives, shards(): lax.psum(lax.psum((jnp.stack(taps), grad_down_part, grad_up_part, column_...  17.3 us
    all_to_all x2, starting transfers between devices, to_coarse(): lax.all_to_all(field, 'frames', split_axis=2, concat_axis=0, tiled=True)  12.7 us
  transfers between devices with their start and end apart: 12, of which 6 were waited for; matrix products, arithmetic and copies ran while one was open for 12% of the time, Pallas kernels for 0%

profile of v1, /device:TPU:0, one launch (start us, length us, event | category | flops | bytes accessed | tf_op | source)
XLA Modules:
  0.0 524.6 jit_solution(10677895231024471858)
XLA Ops:
  7.2 1.9 fusion.68
  9.1 3.1 collective-permute-start
  20.1 7.6 %all-to-all-start.2 = ((bf16[8,2,5120]{2,1,0:T(2,128)(2,1)}), bf16[8,2,5120]{2,1,0:T(2,128)(2,1)}, u32[]{:S(2)}, u32[]{:S(2)}) async-start(bf16[8,2,5120]{2,1,0:T(2,128)(2,1)} %reshape.238), calls=%async_computation.2 | async-start | bytes 327680 | tf_op jit(solution)/shard_map/all_to_all | solution.py:55
  34.0 1.9 reshape.205
  45.7 2.5 reshape_reshape.3
  53.8 5.1 all-to-all-start
  58.9 2.2 reshape.239
  62.1 11.6 %all_gather.7 = bf16[8,4,8,1280]{3,2,0,1:T(8,128)(2,1)S(1)} all-gather(bf16[8,1,8,1280]{3,2,0,1:T(8,128)(2,1)S(1)} %bitcast.199), channel_id=1, replica_groups=mesh['frames'=8,'heads'=4] {'heads'}, dimensions={1}, use_global_device_ids=true | all-gather | bytes 819200 | tf_op jit(solution)/shard_map/all_gather | solution.py:56
  77.6 11.5 %all_gather.6 = bf16[8,4,8,1280]{3,2,0,1:T(8,128)(2,1)S(1)} all-gather(bf16[8,1,8,1280]{3,2,0,1:T(8,128)(2,1)S(1)} %bitcast.200), channel_id=1, replica_groups=mesh['frames'=8,'heads'=4] {'heads'}, dimensions={1}, use_global_device_ids=true | all-gather | bytes 819200 | tf_op jit(solution)/shard_map/all_gather | solution.py:56
  91.8 3.3 reshape.210
  95.1 2.0 fusion.66
  101.2 2.2 fusion.9
  108.4 2.2 convolution_bitcast_fusion.1
  110.6 2.2 convolution_bitcast_fusion.2
  113.8 2.3 convolution_convert_fusion.3
  118.6 2.7 convolution_convert_fusion.2
  122.0 55.8 %all-reduce.17.cloned.1.call-done = (bf16[8,4,8,1280]{3,2,1,0:T(8,128)(2,1)}, bf16[8,4,8,1280]{3,2,1,0:T(8,128)(2,1)}) async-done(((bf16[8,4,8,1280]{3,2,1,0:T(8,128)(2,1)}, bf16[8,4,8,1280]{3,2,1,0:T(8,128)(2,1)}), (bf16[8,4,8,1280]{3,2,1,0:T(8,128)(2,1)}, bf16[8,4,8,1280]{3,2,1,0:T(8,128)(2,1)})) %all-reduce.17.cloned.1.call-update) | async-done | bytes 1310736
  177.8 2.4 fusion.43
  180.2 4.6 all-to-all-start.3
  184.8 2.3 fusion.42
  187.1 4.9 all-to-all-done.3
  192.0 4.0 all-to-all-start.1
  201.2 2.0 all-to-all-done.1
  203.2 2.5 fusion.47
  208.9 2.3 convolution_convert_fusion
  213.0 104.2 %all-reduce.13.cloned.1.call-done = (f32[3,320,320]{2,1,0:T(8,128)}, f32[320,1280]{1,0:T(8,128)}, f32[1280,320]{0,1:T(8,128)}) async-done(((f32[3,320,320]{2,1,0:T(8,128)}, f32[320,1280]{1,0:T(8,128)}, f32[1280,320]{0,1:T(8,128)}), (f32[3,320,320]{2,1,0:T(8,128)}, f32[320,1280]{1,0:T(8,128)}, f32[1280,320]{0,1:T(8,128)})) %all-reduce.13.cloned.1.call-update) | async-done | bytes 4505616 | tf_op jit(solution)/shard_map/psum | solution.py:161
  323.1 9.4 %psum.74 = f32[1280]{0:T(1024)S(1)} all-reduce(f32[1280]{0:T(1024)S(1)} %convert_reduce_fusion.1), channel_id=1, replica_groups=mesh['frames'=8,'heads'=4] {'heads'}, use_global_device_ids=true, to_apply=%region_13.14 | all-reduce | flops 1280 | bytes 10240 | tf_op jit(solution)/shard_map/psum | solution.py:161
  332.5 17.3 %psum.75 = f32[1280]{0:T(1024)S(1)} all-reduce(f32[1280]{0:T(1024)S(1)} %psum.74), channel_id=1, replica_groups=mesh['frames'=8,'heads'=4] {'frames'}, use_global_device_ids=true, to_apply=%region_14.15 | all-reduce | flops 1280 | bytes 10240 | tf_op jit(solution)/shard_map/psum | solution.py:160
  352.0 50.2 %all-reduce.15.cloned.1.call-done = (bf16[1280,960]{0,1:T(8,128)(2,1)}, bf16[320,1280]{1,0:T(8,128)(2,1)}) async-done(((bf16[1280,960]{0,1:T(8,128)(2,1)}, bf16[320,1280]{1,0:T(8,128)(2,1)}), (bf16[1280,960]{0,1:T(8,128)(2,1)}, bf16[320,1280]{1,0:T(8,128)(2,1)})) %all-reduce.15.cloned.1.call-update) | async-done | bytes 3276816 | tf_op jit(solution)/shard_map/psum | solution.py:157
  402.2 4.4 convert_element_type.187
  411.4 100.8 %all-reduce.11.cloned.1.call-done = (f32[3,320,320]{2,1,0:T(8,128)}, f32[320,1280]{1,0:T(8,128)}, f32[1280,320]{0,1:T(8,128)}) async-done(((f32[3,320,320]{2,1,0:T(8,128)}, f32[320,1280]{1,0:T(8,128)}, f32[1280,320]{0,1:T(8,128)}), (f32[3,320,320]{2,1,0:T(8,128)}, f32[320,1280]{1,0:T(8,128)}, f32[1280,320]{0,1:T(8,128)})) %all-reduce.11.cloned.1.call-update) | async-done | bytes 4505616 | tf_op jit(solution)/shard_map/psum | solution.py:160
  512.2 2.7 copy.290
  (198 shorter events, 75.3 us)
Async XLA Ops:
  7.2 82.8 %copy-start = (bf16[1280,960]{0,1:T(8,128)(2,1)S(1)}, bf16[1280,960]{0,1:T(8,128)(2,1)}, u32[]{:S(2)}) copy-start(bf16[1280,960]{0,1:T(8,128)(2,1)} %param.13) | copy-start | bytes 7372804
  9.1 21.3 %collective-permute-start = (bf16[1,2,128,320]{2,3,1,0:T(8,128)(2,1)}, bf16[1,2,128,320]{2,3,1,0:T(8,128)(2,1)}, u32[]{:S(2)}, u32[]{:S(2)}) collective-permute-start(bf16[1,2,128,320]{2,3,1,0:T(8,128)(2,1)} %get-tuple-element.76), channel_id=1, source_target_pairs={{0,4},{4,8},{8,12},{12,16},{16,20},{20,24},{24,28},{1,5},{5,9},{9,... | collective-permute-start | bytes 491528 | tf_op jit(solution)/shard_map/ppermute | solution.py:18
  12.1 23.8 %collective-permute-start.1 = (bf16[1,2,128,320]{2,3,1,0:T(8,128)(2,1)}, bf16[1,2,128,320]{2,3,1,0:T(8,128)(2,1)}, u32[]{:S(2)}, u32[]{:S(2)}) collective-permute-start(bf16[1,2,128,320]{2,3,1,0:T(8,128)(2,1)} %get-tuple-element.75), channel_id=1, source_target_pairs={{4,0},{8,4},{12,8},{16,12},{20,16},{24,20},{28,24},{5,1},{9,5},{13... | collective-permute-start | bytes 491528 | tf_op jit(solution)/shard_map/ppermute | solution.py:20
  14.6 13.9 %copy-start.6 = (bf16[2,2,128,320]{2,3,1,0:T(8,128)(2,1)S(1)}, bf16[2,2,128,320]{2,3,1,0:T(8,128)(2,1)}, u32[]{:S(2)}) copy-start(bf16[2,2,128,320]{2,3,1,0:T(8,128)(2,1)} %param.9) | copy-start | bytes 983044
  20.1 33.7 %all-to-all-start.2 = ((bf16[8,2,5120]{2,1,0:T(2,128)(2,1)}), bf16[8,2,5120]{2,1,0:T(2,128)(2,1)}, u32[]{:S(2)}, u32[]{:S(2)}) async-start(bf16[8,2,5120]{2,1,0:T(2,128)(2,1)} %reshape.238), calls=%async_computation.2 | async-start | bytes 327680 | tf_op jit(solution)/shard_map/all_to_all | solution.py:55
  34.0 7.4 %copy-start.12 = (bf16[3,320,320]{2,1,0:T(8,128)(2,1)S(1)}, bf16[3,320,320]{2,1,0:T(8,128)(2,1)}, u32[]{:S(2)}) copy-start(bf16[3,320,320]{2,1,0:T(8,128)(2,1)} %param.10) | copy-start | bytes 1843204
  44.5 5.2 copy-start.4
  49.7 4.1 copy-start.36
  53.8 22.3 %all-to-all-start = ((bf16[8,2,5120]{2,1,0:T(2,128)(2,1)}), bf16[8,2,5120]{2,1,0:T(2,128)(2,1)}, u32[]{:S(2)}, u32[]{:S(2)}) async-start(bf16[8,2,5120]{2,1,0:T(2,128)(2,1)} %reshape.236), calls=%async_computation | async-start | bytes 327680 | tf_op jit(solution)/shard_map/all_to_all | solution.py:55
  58.9 15.7 %copy-start.8 = (bf16[320,1280]{1,0:T(8,128)(2,1)S(1)}, bf16[320,1280]{1,0:T(8,128)(2,1)}, u32[]{:S(2)}) copy-start(bf16[320,1280]{1,0:T(8,128)(2,1)} %param.14) | copy-start | bytes 2457604
  58.9 118.9 %all-reduce.17.cloned.1.call-start = ((), (), s32[]{:S(2)}) async-start(), calls=%async_computation.7 | async-start | bytes 2621440
  77.5 13.2 %copy-start.14 = (bf16[64,1,1,1280]{3,2,1,0:T(2,128)(2,1)}, bf16[64,1,1,1280]{3,2,1,0:T(2,128)(2,1)S(1)}, u32[]{:S(2)}) copy-start(bf16[64,1,1,1280]{3,2,1,0:T(2,128)(2,1)S(1)} %reshape.237) | copy-start | bytes 491524
  98.1 5.3 %copy-start.21 = (bf16[8,32,4,80]{3,2,1,0:T(4,128)(2,1)S(1)}, bf16[8,32,4,80]{3,2,1,0:T(4,128)(2,1)}, u32[]{:S(2)}) copy-start(bf16[8,32,4,80]{3,2,1,0:T(4,128)(2,1)} %reshape.214) | copy-start | bytes 491524
  101.1 3.3 copy-start.25
  107.0 6.8 %copy-start.9 = (bf16[320,1280]{1,0:T(8,128)(2,1)S(1)}, bf16[320,1280]{1,0:T(8,128)(2,1)}, u32[]{:S(2)}) copy-start(bf16[320,1280]{1,0:T(8,128)(2,1)} %param.14) | copy-start | bytes 2457604
  108.4 4.4 copy-start.32
  112.9 3.2 copy-start.19
  121.3 63.4 %copy-start.15 = (bf16[64,1,1,1280]{3,2,1,0:T(2,128)(2,1)S(1)}, bf16[64,1,1,1280]{3,2,1,0:T(2,128)(2,1)}, u32[]{:S(2)}) copy-start(bf16[64,1,1,1280]{3,2,1,0:T(2,128)(2,1)} %copy-done.14) | copy-start | bytes 491524
  121.3 74.9 %copy-start.10 = (bf16[320,1280]{1,0:T(8,128)(2,1)S(1)}, bf16[320,1280]{1,0:T(8,128)(2,1)}, u32[]{:S(2)}) copy-start(bf16[320,1280]{1,0:T(8,128)(2,1)} %param.11) | copy-start | bytes 2457604
  180.2 11.8 %all-to-all-start.3 = ((bf16[8,1,8,1280]{3,2,1,0:T(8,128)(2,1)}), bf16[8,1,8,1280]{3,2,1,0:T(8,128)(2,1)S(1)}, u32[]{:S(2)}, u32[]{:S(2)}) async-start(bf16[8,1,8,1280]{3,2,1,0:T(8,128)(2,1)} %fusion.43), calls=%async_computation.3 | async-start | bytes 327680 | tf_op jit(solution)/shard_map/all_to_all | solution.py:67
  184.8 12.2 %copy-start.30 = (bf16[2,2,128,320]{2,3,1,0:T(8,128)(2,1)S(1)}, bf16[2,2,128,320]{2,3,1,0:T(8,128)(2,1)}, u32[]{:S(2)}) copy-start(bf16[2,2,128,320]{2,3,1,0:T(8,128)(2,1)} %param.17) | copy-start | bytes 983044
  187.1 10.0 %copy-start.16 = (bf16[3,2,128,320]{2,3,1,0:T(8,128)(2,1)S(1)}, bf16[3,2,128,320]{2,3,1,0:T(8,128)(2,1)}, u32[]{:S(2)}) copy-start(bf16[3,2,128,320]{2,3,1,0:T(8,128)(2,1)} %constant_dynamic-update-slice_fusion.2) | copy-start | bytes 1474564
  192.0 11.2 %all-to-all-start.1 = ((bf16[8,1,8,1280]{3,2,1,0:T(8,128)(2,1)}), bf16[8,1,8,1280]{3,2,1,0:T(8,128)(2,1)}, u32[]{:S(2)}, u32[]{:S(2)}) async-start(bf16[8,1,8,1280]{3,2,1,0:T(8,128)(2,1)} %fusion.42), calls=%async_computation.1 | async-start | bytes 327680 | tf_op jit(solution)/shard_map/all_to_all | solution.py:67
  196.0 121.3 %all-reduce.13.cloned.1.call-start = ((), (), s32[]{:S(2)}) async-start(), calls=%async_computation.5 | async-start | bytes 9502720 | tf_op jit(solution)/shard_map/psum | solution.py:161
  199.6 3.6 copy-start.40
  205.7 3.2 copy-start.18
  205.7 196.5 %all-reduce.15.cloned.1.call-start = ((), (), s32[]{:S(2)}) async-start(), calls=%async_computation.6 | async-start | bytes 6553600 | tf_op jit(solution)/shard_map/psum | solution.py:157
  211.2 301.0 %all-reduce.11.cloned.1.call-start = ((), (), s32[]{:S(2)}) async-start(), calls=%async_computation.4 | async-start | bytes 9502720 | tf_op jit(solution)/shard_map/psum | solution.py:160
  320.0 87.8 %collective-permute-start.3 = (bf16[1,2,128,320]{2,3,1,0:T(8,128)(2,1)S(1)}, bf16[1,2,128,320]{2,3,1,0:T(8,128)(2,1)S(1)}, u32[]{:S(2)}, u32[]{:S(2)}) collective-permute-start(bf16[1,2,128,320]{2,3,1,0:T(8,128)(2,1)S(1)} %get-tuple-element.73), channel_id=1, source_target_pairs={{0,4},{4,8},{8,12},{12,16},{16,20},{20,24},{24,28},{1,5},{5,9},{9,... | collective-permute-start | bytes 491528 | tf_op jit(solution)/shard_map/ppermute | solution.py:18
  321.6 86.3 %collective-permute-start.2 = (bf16[1,2,128,320]{2,3,1,0:T(8,128)(2,1)S(1)}, bf16[1,2,128,320]{2,3,1,0:T(8,128)(2,1)S(1)}, u32[]{:S(2)}, u32[]{:S(2)}) collective-permute-start(bf16[1,2,128,320]{2,3,1,0:T(8,128)(2,1)S(1)} %get-tuple-element.74), channel_id=1, source_target_pairs={{4,0},{8,4},{12,8},{16,12},{20,16},{24,20},{28,24},{5,1},{9,5},{13... | collective-permute-start | bytes 491528 | tf_op jit(solution)/shard_map/ppermute | solution.py:20
  402.2 4.4 copy-start.38
  514.9 3.2 copy-start.1
  (23 other events, 33.5 us)
Sparse Core Ops, SparseCore 0:
  121.5 56.2 all-reduce.16
  205.8 111.3 all-reduce.12
  320.3 81.9 all-reduce.14
  404.7 107.4 all-reduce.10
